TPU v7x, 32 devices: a whole 2x2x4 slice. The times are simulated.
32 devices in a mesh: band: 2 (over core), grid: 16 (over z, y, x).
Axes of the slice: x: 2, y: 2, z: 4, core: 2. Of those that a mesh axis runs over, the one named last changes fastest.
Arguments:
- coefficients: float32 [4, 2, 128, 128, 128], P('band', None, 'grid'), may hold values from -0.01171875 to 0.01171875
- potential: float32 [128, 128, 128], P('grid'), may hold values from -3 to 3
- external: float32 [128, 128, 128], P('grid'), may hold values from -6 to 6
- core_density: float32 [128, 128, 128], P('grid'), may hold values from 0.05 to 0.5
- rotations: float32 [2, 4, 2], P(None, 'band'), may hold values from -2 to 3
- mlp_in: float32 [3, 32], replicated, may hold values from -4 to 4
- mlp_out: float32 [32], replicated, may hold values from -0.4 to 0.4
Outputs:
- new_coefficients: float32 [4, 2, 128, 128, 128], P('band', None, 'grid')
- new_potential: float32 [128, 128, 128], P('grid')
All inputs are finite; a program needn't handle non-finite values.
Results may differ from a plain program's by a relative error of at most 0.0003.
Values sent between devices are 32-bit elements; how exact they have to be, the bound alone decides.
A program may use at most 64 MiB of HBM per device.

v0:
```python
import math
import jax
import jax.numpy as jnp
from jax import lax
from jax.sharding import PartitionSpec as P

NX = 128
NY = 128
NZ = 128
ITERS = 2
step_size = 0.2
epsilon = 1e-06
spacing = 0.58
kinetic_scale = 0.5 * (2.0 * math.pi / spacing) ** 2
coulomb_scale = spacing * spacing / math.pi
gradient_scale = 2.0 * math.pi / spacing
reduced_scale = 2.0 * (3.0 * math.pi * math.pi) ** (1.0 / 3.0)
exchange_scale = (3.0 / math.pi) ** (1.0 / 3.0)


def frequencies(points, offset, length):
    places = offset + lax.iota(jnp.int32, length)
    return jnp.where(2 * places < points, places, places - points)


def without_nyquist(values, points):
    return jnp.where(2 * values == -points, 0, values)


def reciprocal_tables(offset, length):
    along_x = frequencies(NX, offset, length)
    along_y = frequencies(NY, 0, NY)
    raw_z = frequencies(NZ, 0, NZ)
    along_z = raw_z * (NX // NZ)
    squared = (
        along_x[:, None, None] * along_x[:, None, None]
        + along_y[None, :, None] * along_y[None, :, None]
        + along_z[None, None, :] * along_z[None, None, :]
    )
    cutoff = (16 * squared <= NX * NX).astype(jnp.float32)
    kinetic = kinetic_scale * squared.astype(jnp.float32) / (NX * NX)
    coulomb = jnp.where(
        squared > 0, coulomb_scale * (NX * NX) / jnp.maximum(squared, 1).astype(jnp.float32), 0.0
    )
    slope_x = gradient_scale * without_nyquist(along_x, NX).astype(jnp.float32) / NX
    slope_y = gradient_scale * without_nyquist(along_y, NY).astype(jnp.float32) / NX
    slope_z = gradient_scale * (without_nyquist(raw_z, NZ) * (NX // NZ)).astype(jnp.float32) / NX
    return (
        cutoff,
        kinetic,
        coulomb,
        slope_x[:, None, None],
        slope_y[None, :, None],
        slope_z[None, None, :],
    )


def dft_tables(points, direction):
    places = lax.iota(jnp.int32, points)
    phases = places[:, None] * places[None, :] % points
    angles = phases.astype(jnp.float32) * (2.0 * math.pi / points)
    return (jnp.cos(angles), direction * jnp.sin(angles))


def transform(perceptron_levels, tables, pattern):
    highest = lax.Precision.HIGHEST
    cosine_table, sine_table = tables
    real_part = perceptron_levels[:, 0]
    imag_part = perceptron_levels[:, 1]
    new_real = jnp.einsum(pattern, real_part, cosine_table, precision=highest) - jnp.einsum(
        pattern, imag_part, sine_table, precision=highest
    )
    new_imag = jnp.einsum(pattern, real_part, sine_table, precision=highest) + jnp.einsum(
        pattern, imag_part, cosine_table, precision=highest
    )
    return jnp.stack([new_real, new_imag], 1)


def toward_position_grid(spectral_amplitude, fourier_synthesis, orbital_holder):
    perceptron_levels = transform(spectral_amplitude, fourier_synthesis[2], "bxyz,zw->bxyw")
    perceptron_levels = transform(perceptron_levels, fourier_synthesis[1], "bxyz,yv->bxvz")
    perceptron_levels = orbital_holder(perceptron_levels)
    return transform(perceptron_levels, fourier_synthesis[0], "bxyz,xu->byuz")


def toward_spectral_amplitudes(position_grid_values, fourier_analysis, orbital_holder):
    perceptron_levels = transform(position_grid_values, fourier_analysis[0], "byxz,xu->buyz")
    perceptron_levels = orbital_holder(perceptron_levels)
    perceptron_levels = transform(perceptron_levels, fourier_analysis[1], "bxyz,yv->bxvz")
    perceptron_levels = transform(perceptron_levels, fourier_analysis[2], "bxyz,zw->bxyw")
    return perceptron_levels / (NX * NY * NZ)


def body(coefficients, potential, external, core_density, rotations, mlp_in, mlp_out):
    highest = lax.Precision.HIGHEST
    planes = coefficients.shape[2]
    offset = lax.axis_index("grid") * planes
    cutoff, kinetic, coulomb, slope_x, slope_y, slope_z = reciprocal_tables(offset, planes)
    fourier_synthesis = (dft_tables(NX, 1.0), dft_tables(NY, 1.0), dft_tables(NZ, 1.0))
    fourier_analysis = (dft_tables(NX, -1.0), dft_tables(NY, -1.0), dft_tables(NZ, -1.0))

    def outward(perceptron_levels):
        return lax.all_to_all(perceptron_levels, "grid", split_axis=3, concat_axis=2, tiled=True)

    def inward(perceptron_levels):
        return lax.all_to_all(perceptron_levels, "grid", split_axis=2, concat_axis=3, tiled=True)

    current = cutoff * coefficients
    for iteration in range(ITERS):
        applied = cutoff * (
            kinetic * current
            + toward_spectral_amplitudes(
                toward_position_grid(current, fourier_synthesis, outward) * potential,
                fourier_analysis,
                inward,
            )
        )
        rotation = rotations[iteration]
        intersection, energy = lax.psum(
            (
                jnp.sum(current * current, axis=(1, 2, 3, 4)),
                jnp.sum(current * applied, axis=(1, 2, 3, 4)),
            ),
            "grid",
        )
        factor = 1.0 + step_size * (energy / (intersection + epsilon))
        updated = factor[:, None, None, None, None] * current - step_size * applied
        updated = jnp.einsum("ij,jcxyz->icxyz", rotation, updated, precision=highest)
        length = lax.psum(jnp.sum(updated * updated, axis=(1, 2, 3, 4)), "grid")
        current = updated / jnp.sqrt(length + epsilon)[:, None, None, None, None]
    real_space = toward_position_grid(current, fourier_synthesis, outward)
    bands_all = coefficients.shape[0] * lax.axis_size("band")
    partial_value = 2.0 / bands_all * jnp.sum(real_space * real_space, axis=(0, 1))
    density = lax.psum(partial_value, "band") + core_density
    spectrum = toward_spectral_amplitudes(
        jnp.stack([density, jnp.zeros_like(density)])[None], fourier_analysis, inward
    )[0]
    spec_real = spectrum[0]
    spec_imag = spectrum[1]
    first_real = coulomb * spec_real - slope_x * spec_real
    first_imag = coulomb * spec_imag - slope_x * spec_imag
    second_real = -slope_y * spec_imag - slope_z * spec_real
    second_imag = slope_y * spec_real - slope_z * spec_imag
    fields = toward_position_grid(
        jnp.stack([jnp.stack([first_real, first_imag]), jnp.stack([second_real, second_imag])]),
        fourier_synthesis,
        outward,
    )
    hartree = fields[0, 0]
    change_x = fields[0, 1]
    change_y = fields[1, 0]
    change_z = fields[1, 1]
    cube_root = jnp.cbrt(density)
    gradient = jnp.sqrt(change_x * change_x + change_y * change_y + change_z * change_z)
    reduced = gradient / (reduced_scale * density * cube_root)
    bounded = reduced / (1.0 + reduced)
    hidden = jnp.tanh(
        mlp_in[0][:, None, None, None] * cube_root
        + mlp_in[1][:, None, None, None] * bounded
        + mlp_in[2][:, None, None, None]
    )
    enhance = 1.0 + jnp.einsum("k,kyxz->yxz", mlp_out, hidden, precision=highest)
    new_potential = external + hartree - exchange_scale * cube_root * enhance
    return (current, new_potential)


def solution(mesh):
    in_specs = (
        P("band", None, "grid", None, None),
        P("grid", None, None),
        P("grid", None, None),
        P("grid", None, None),
        P(None, "band", None),
        P(),
        P(),
    )
    out_specs = (P("band", None, "grid", None, None), P("grid", None, None))
    return jax.shard_map(body, mesh=mesh, in_specs=in_specs, out_specs=out_specs, check_vma=False)
```

profile of v0, /device:TPU:12, one launch (start us, length us, event | category | flops | bytes accessed | tf_op | source)
XLA Modules:
  0.0 682.6 jit_solution(3617643584464941430)
XLA Ops:
  7.5 1.9 copy_multiply_fusion
  18.2 1.3 fusion.39
  21.0 54.6 %all_to_all.126 = f32[2,2,8,128,128]{4,2,0,1,3:T(8,128)S(1)} all-to-all(f32[2,2,8,128,128]{4,2,0,1,3:T(8,128)S(1)} %copy.58), channel_id=1, replica_groups=mesh['band'=2,'grid'=16] {'grid'}, dimensions={3} | all-to-all | bytes 4194304 | tf_op jit(solution)/shard_map/all_to_all | solution.py:103
  78.4 1.3 fusion.36
  79.8 1.4 fusion.37
  84.0 1.3 fusion.34
  85.3 1.3 fusion.35
  86.8 2.5 copy.60
  89.4 16.6 %all-to-all-start.1 = ((f32[2,2,128,8,128]{4,3,0,1,2:T(8,128)}), f32[2,2,128,8,128]{4,3,0,1,2:T(8,128)S(1)}, u32[]{:S(2)}, u32[]{:S(2)}) async-start(f32[2,2,128,8,128]{4,3,0,1,2:T(8,128)} %copy.60), calls=%async_computation.1 | async-start | bytes 4194304 | tf_op jit(solution)/shard_map/all_to_all | solution.py:106
  106.2 46.5 %all-to-all-done.1 = f32[2,2,128,8,128]{4,3,0,1,2:T(8,128)S(1)} async-done(((f32[2,2,128,8,128]{4,3,0,1,2:T(8,128)}), f32[2,2,128,8,128]{4,3,0,1,2:T(8,128)S(1)}, u32[]{:S(2)}, u32[]{:S(2)}) %all-to-all-start.1) | async-done | bytes 2097184 | tf_op jit(solution)/shard_map/all_to_all | solution.py:106
  164.8 29.5 %all-reduce.2 = (f32[2]{0:T(128)S(1)}, f32[2]{0:T(128)S(1)}) all-reduce(f32[2]{0:T(128)S(1)} %get-tuple-element.9, f32[2]{0:T(128)S(1)} %get-tuple-element.8), channel_id=1, replica_groups=mesh['band'=2,'grid'=16] {'grid'}, use_global_device_ids=true, to_apply=%region_1.2 | all-reduce | flops 4 | bytes 32 | tf_op jit(solution)/shard_map/psum | solution.py:119
  194.3 2.3 multiply_subtract_fusion.1
  196.7 9.5 %multiply_reduce_fusion.3 = (f32[2]{0:T(128)S(1)}, f32[2,8,128,128,2]{3,4,2,1,0:T(2,128)S(1)}) fusion(f32[2,2,2]{2,1,0:T(2,128)S(1)} %copy-done.11, f32[2,2,8,128,128]{4,3,2,0,1:T(8,128)S(1)} %multiply_subtract_fusion.1), kind=kOutput, calls=%fused_computation.35 | convolution fusion | flops 13631486 | bytes 4195336 | tf_op jit(solution)/shard_map/ij,jcxyz->icxyz/dot_general | solution.py:128
  206.1 37.0 %psum.51 = f32[2]{0:T(128)S(1)} all-reduce(f32[2]{0:T(128)S(1)} %get-tuple-element.27), channel_id=1, replica_groups=mesh['band'=2,'grid'=16] {'grid'}, use_global_device_ids=true, to_apply=%region_5.6 | all-reduce | flops 2 | bytes 16 | tf_op jit(solution)/shard_map/psum | solution.py:129
  251.0 1.3 fusion.28
  252.3 1.3 fusion.29
  255.1 44.4 %all_to_all.127 = f32[2,2,8,128,128]{4,2,0,1,3:T(8,128)S(1)} all-to-all(f32[2,2,8,128,128]{4,2,0,1,3:T(8,128)S(1)} %copy.72), channel_id=1, replica_groups=mesh['band'=2,'grid'=16] {'grid'}, dimensions={3} | all-to-all | bytes 4194304 | tf_op jit(solution)/shard_map/all_to_all | solution.py:103
  302.4 1.3 fusion.26
  303.7 1.4 fusion.27
  307.9 1.3 fusion.24
  309.3 1.3 fusion.25
  312.0 45.8 %all_to_all.128 = f32[2,2,128,8,128]{4,3,0,1,2:T(8,128)S(1)} all-to-all(f32[2,2,128,8,128]{4,3,0,1,2:T(8,128)S(1)} %copy.74), channel_id=1, replica_groups=mesh['band'=2,'grid'=16] {'grid'}, dimensions={2} | all-to-all | bytes 4194304 | tf_op jit(solution)/shard_map/all_to_all | solution.py:106
  369.3 29.9 %all-reduce.1 = (f32[2]{0:T(128)S(1)}, f32[2]{0:T(128)S(1)}) all-reduce(f32[2]{0:T(128)S(1)} %get-tuple-element.7, f32[2]{0:T(128)S(1)} %get-tuple-element.6), channel_id=1, replica_groups=mesh['band'=2,'grid'=16] {'grid'}, use_global_device_ids=true, to_apply=%region_7.8 | all-reduce | flops 4 | bytes 32 | tf_op jit(solution)/shard_map/psum | solution.py:119
  399.1 2.3 multiply_subtract_fusion
  401.4 9.9 %multiply_reduce_fusion = (f32[2]{0:T(128)S(1)}, f32[2,8,128,128,2]{3,4,2,1,0:T(2,128)}) fusion(f32[2,2,2]{2,1,0:T(2,128)S(1)} %copy-done.11, f32[2,2,8,128,128]{4,3,2,0,1:T(8,128)S(1)} %multiply_subtract_fusion), kind=kOutput, calls=%fused_computation.31 | convolution fusion | flops 13631486 | bytes 4195336 | tf_op jit(solution)/shard_map/ij,jcxyz->icxyz/dot_general | solution.py:128
  411.3 36.7 %psum.54 = f32[2]{0:T(128)S(1)} all-reduce(f32[2]{0:T(128)S(1)} %get-tuple-element.29), channel_id=1, replica_groups=mesh['band'=2,'grid'=16] {'grid'}, use_global_device_ids=true, to_apply=%region_11.12 | all-reduce | flops 2 | bytes 16 | tf_op jit(solution)/shard_map/psum | solution.py:129
  448.0 2.6 divide_bitcast_fusion
  458.3 1.3 fusion.19
  461.1 1.4 copy.89
  462.6 44.1 %all_to_all.129 = f32[2,2,8,128,128]{4,2,0,1,3:T(8,128)S(1)} all-to-all(f32[2,2,8,128,128]{4,2,0,1,3:T(8,128)S(1)} %copy.89), channel_id=1, replica_groups=mesh['band'=2,'grid'=16] {'grid'}, dimensions={3} | all-to-all | bytes 4194304 | tf_op jit(solution)/shard_map/all_to_all | solution.py:103
  509.5 1.3 fusion.16
  510.8 1.3 fusion.17
  513.2 18.1 %all-reduce.5.cloned.1.call-done = f32[8,128,128]{2,1,0:T(8,128)} async-done(((f32[8,128,128]{2,1,0:T(8,128)}), f32[8,128,128]{2,1,0:T(8,128)}) %all-reduce.5.cloned.1.call-update) | async-done | bytes 524304 | tf_op jit(solution)/shard_map/psum | solution.py:134
  531.3 2.3 fusion.639
  537.2 1.6 copy.91
  538.7 7.3 %all-to-all-start.5 = ((f32[1,2,128,8,128]{4,3,1,0,2:T(8,128)}), f32[1,2,128,8,128]{4,3,1,0,2:T(8,128)}, u32[]{:S(2)}, u32[]{:S(2)}) async-start(f32[1,2,128,8,128]{4,3,1,0,2:T(8,128)} %copy.91), calls=%async_computation.5 | async-start | bytes 2097152 | tf_op jit(solution)/shard_map/all_to_all | solution.py:106
  546.1 25.3 %all-to-all-done.5 = f32[1,2,128,8,128]{4,3,1,0,2:T(8,128)} async-done(((f32[1,2,128,8,128]{4,3,1,0,2:T(8,128)}), f32[1,2,128,8,128]{4,3,1,0,2:T(8,128)}, u32[]{:S(2)}, u32[]{:S(2)}) %all-to-all-start.5) | async-done | bytes 1048608 | tf_op jit(solution)/shard_map/all_to_all | solution.py:106
  571.4 1.3 copy.211
  584.0 1.5 fusion.137
  588.0 1.3 fusion.15
  590.8 2.5 copy.101
  593.3 5.9 all-to-all-start.6
  599.3 1.6 copy.103
  600.9 45.7 %all-to-all-done.6 = f32[2,2,8,128,128]{4,2,0,1,3:T(8,128)} async-done(((f32[2,2,8,128,128]{4,2,0,1,3:T(8,128)}), f32[2,2,8,128,128]{4,2,0,1,3:T(8,128)}, u32[]{:S(2)}, u32[]{:S(2)}) %all-to-all-start.6) | async-done | bytes 2097184 | tf_op jit(solution)/shard_map/all_to_all | solution.py:103
  646.6 1.8 copy.205
  652.3 1.4 fusion.13
  654.4 4.3 add_tanh_fusion
  658.8 15.2 %fusion = f32[1,8,128,128]{3,0,2,1:T(1,128)S(1)} fusion(f32[32,8,128,128]{3,2,1,0:T(8,128)S(1)} %add_tanh_fusion, f32[32]{0:T(128)S(1)} %copy-done), kind=kOutput, calls=%fused_computation | convolution fusion | flops 50331648 | bytes 17301632 | tf_op jit(solution)/shard_map/k,kyxz->yxz/dot_general | solution.py:162
  (135 shorter events, 93.9 us)
Async XLA Ops:
  7.2 651.6 %copy-start = (f32[32]{0:T(128)S(1)}, f32[32]{0:T(128)}, u32[]{:S(2)}) copy-start(f32[32]{0:T(128)} %param.13) | copy-start | bytes 388
  79.8 1.4 copy-start.6
  89.4 63.3 %all-to-all-start.1 = ((f32[2,2,128,8,128]{4,3,0,1,2:T(8,128)}), f32[2,2,128,8,128]{4,3,0,1,2:T(8,128)S(1)}, u32[]{:S(2)}, u32[]{:S(2)}) async-start(f32[2,2,128,8,128]{4,3,0,1,2:T(8,128)} %copy.60), calls=%async_computation.1 | async-start | bytes 4194304 | tf_op jit(solution)/shard_map/all_to_all | solution.py:106
  106.0 425.3 %all-reduce.5.cloned.1.call-start = ((), (), s32[]{:S(2)}) async-start(), calls=%async_computation.7 | async-start | bytes 1048576 | tf_op jit(solution)/shard_map/psum | solution.py:134
  161.9 2.9 copy-start.4
  161.9 2.0 copy-start.1
  163.9 1.0 copy-start.5
  194.3 2.3 copy-start.11
  303.7 1.4 copy-start.7
  366.9 2.3 copy-start.2
  368.2 1.1 copy-start.3
  512.1 19.1 %copy-start.9 = (f32[8,128,128]{2,1,0:T(8,128)S(1)}, f32[8,128,128]{2,1,0:T(8,128)}, u32[]{:S(2)}) copy-start(f32[8,128,128]{2,1,0:T(8,128)} %param.10) | copy-start | bytes 1572868
  538.7 32.7 %all-to-all-start.5 = ((f32[1,2,128,8,128]{4,3,1,0,2:T(8,128)}), f32[1,2,128,8,128]{4,3,1,0,2:T(8,128)}, u32[]{:S(2)}, u32[]{:S(2)}) async-start(f32[1,2,128,8,128]{4,3,1,0,2:T(8,128)} %copy.91), calls=%async_computation.5 | async-start | bytes 2097152 | tf_op jit(solution)/shard_map/all_to_all | solution.py:106
  593.3 6.0 copy-start.10
  593.3 53.2 %all-to-all-start.6 = ((f32[2,2,8,128,128]{4,2,0,1,3:T(8,128)}), f32[2,2,8,128,128]{4,2,0,1,3:T(8,128)}, u32[]{:S(2)}, u32[]{:S(2)}) async-start(f32[2,2,8,128,128]{4,2,0,1,3:T(8,128)} %copy.101), calls=%async_computation.6 | async-start | bytes 4194304 | tf_op jit(solution)/shard_map/all_to_all | solution.py:103
  658.8 15.3 %copy-start.8 = (f32[8,128,128]{2,1,0:T(8,128)S(1)}, f32[8,128,128]{2,1,0:T(8,128)}, u32[]{:S(2)}) copy-start(f32[8,128,128]{2,1,0:T(8,128)} %param.9) | copy-start | bytes 1572868
Sparse Core Ops, SparseCore 0:
  513.3 17.9 all-reduce.4
where the time goes:
time: 692 us; the launch traced here: 683 us
  blocking collectives  322 us (47%)
  matrix products  137 us (20%)
  waiting for transfers between devices  136 us (20%)
  starting transfers between devices  29.9 us (4%)
  other arithmetic  24 us (3%)
  local copies, waits for them, and re-layouts  18.7 us (3%)
  between operations  15.6 us (2%)
    all_to_all x3, blocking collectives, outward(): lax.all_to_all(perceptron_levels, 'grid', split_axis=3, concat_axis=2, ti...  143 us
    psum x2, blocking collectives, body(): length = lax.psum(jnp.sum(updated * updated, axis=(1, 2, 3, 4)), 'grid')  73.7 us
    all_to_all x2, waiting for transfers between devices, inward(): lax.all_to_all(perceptron_levels, 'grid', split_axis=2, concat_axis=3, ti...  71.8 us
    psum x2, blocking collectives, body(): lax.psum((jnp.sum(current * current, axis=(1, 2, 3, 4)), jnp.sum(current...  59.3 us
    all_to_all x1, blocking collectives, inward(): lax.all_to_all(perceptron_levels, 'grid', split_axis=2, concat_axis=3, ti...  45.8 us
    all_to_all x1, waiting for transfers between devices, outward(): lax.all_to_all(perceptron_levels, 'grid', split_axis=3, concat_axis=2, ti...  45.7 us
    dot_general x21, matrix products, transform(): jnp.einsum(pattern, imag_part, sine_table, precision=highest)  25.9 us
    dot_general x21, matrix products, transform(): jnp.einsum(pattern, imag_part, cosine_table, precision=highest)  25.7 us
  transfers between devices with their start and end apart: 4, of which 4 were waited for; matrix products, arithmetic and copies ran while one was open for 0% of the time, Pallas kernels for 0%

commit v1 on v0

--- a/solution.py
+++ b/solution.py
@@ -126,7 +126,9 @@
         factor = 1.0 + step_size * (energy / (intersection + epsilon))
         updated = factor[:, None, None, None, None] * current - step_size * applied
         updated = jnp.einsum("ij,jcxyz->icxyz", rotation, updated, precision=highest)
-        length = lax.psum(jnp.sum(updated * updated, axis=(1, 2, 3, 4)), "grid")
+        length = jnp.sum(
+            lax.all_gather(jnp.sum(updated * updated, axis=(1, 2, 3, 4)), "grid"), axis=0
+        )
         current = updated / jnp.sqrt(length + epsilon)[:, None, None, None, None]
     real_space = toward_position_grid(current, fourier_synthesis, outward)
     bands_all = coefficients.shape[0] * lax.axis_size("band")

time: 692 us -> 693 us (level)
    psum x2 -> x0, blocking collectives: 73.7 us -> none  [body(): length = lax.psum(jnp.sum(updated * updated, axis=(1, 2, 3, 4)), 'grid')]
    unnamed x0 -> x2, blocking collectives: none -> 73.6 us
where the time goes in v1:
time: 693 us; the launch traced here: 684 us
  blocking collectives  322 us (46%)
  matrix products  137 us (20%)
  waiting for transfers between devices  134 us (19%)
  starting transfers between devices  30.2 us (4%)
  other arithmetic  24.1 us (3%)
  local copies, waits for them, and re-layouts  20 us (3%)
  between operations  16.3 us (2%)
    all_to_all x3, blocking collectives, outward(): lax.all_to_all(perceptron_levels, 'grid', split_axis=3, concat_axis=2, ti...  143 us
    unnamed x2, blocking collectives  73.6 us
    all_to_all x2, waiting for transfers between devices, inward(): lax.all_to_all(perceptron_levels, 'grid', split_axis=2, concat_axis=3, ti...  70.6 us
    psum x2, blocking collectives, body(): lax.psum((jnp.sum(current * current, axis=(1, 2, 3, 4)), jnp.sum(current...  59.4 us
    all_to_all x1, blocking collectives, inward(): lax.all_to_all(perceptron_levels, 'grid', split_axis=2, concat_axis=3, ti...  45.8 us
    all_to_all x1, waiting for transfers between devices, outward(): lax.all_to_all(perceptron_levels, 'grid', split_axis=3, concat_axis=2, ti...  45.7 us
    dot_general x21, matrix products, transform(): jnp.einsum(pattern, imag_part, sine_table, precision=highest)  25.9 us
    dot_general x21, matrix products, transform(): jnp.einsum(pattern, imag_part, cosine_table, precision=highest)  25.7 us
  transfers between devices with their start and end apart: 4, of which 4 were waited for; matrix products, arithmetic and copies ran while one was open for 0% of the time, Pallas kernels for 0%

profile of v1, /device:TPU:12, one launch (start us, length us, event | category | flops | bytes accessed | tf_op | source)
XLA Modules:
  0.0 683.6 jit_solution(1049503798585917079)
XLA Ops:
  7.5 1.9 copy_multiply_fusion
  18.2 1.3 fusion.39
  21.0 54.6 %all_to_all.126 = f32[2,2,8,128,128]{4,2,0,1,3:T(8,128)S(1)} all-to-all(f32[2,2,8,128,128]{4,2,0,1,3:T(8,128)S(1)} %copy.102), channel_id=1, replica_groups=mesh['band'=2,'grid'=16] {'grid'}, dimensions={3} | all-to-all | bytes 4194304 | tf_op jit(solution)/shard_map/all_to_all | solution.py:103
  78.4 1.3 fusion.36
  79.8 1.4 fusion.37
  84.0 1.3 fusion.34
  85.3 1.3 fusion.35
  86.8 2.5 copy.104
  89.4 16.9 %all-to-all-start.1 = ((f32[2,2,128,8,128]{4,3,0,1,2:T(8,128)}), f32[2,2,128,8,128]{4,3,0,1,2:T(8,128)S(1)}, u32[]{:S(2)}, u32[]{:S(2)}) async-start(f32[2,2,128,8,128]{4,3,0,1,2:T(8,128)} %copy.104), calls=%async_computation.1 | async-start | bytes 4194304 | tf_op jit(solution)/shard_map/all_to_all | solution.py:106
  107.8 45.3 %all-to-all-done.1 = f32[2,2,128,8,128]{4,3,0,1,2:T(8,128)S(1)} async-done(((f32[2,2,128,8,128]{4,3,0,1,2:T(8,128)}), f32[2,2,128,8,128]{4,3,0,1,2:T(8,128)S(1)}, u32[]{:S(2)}, u32[]{:S(2)}) %all-to-all-start.1) | async-done | bytes 2097184 | tf_op jit(solution)/shard_map/all_to_all | solution.py:106
  165.1 29.5 %all-reduce.4 = (f32[2]{0:T(128)S(1)}, f32[2]{0:T(128)S(1)}) all-reduce(f32[2]{0:T(128)S(1)} %get-tuple-element.11, f32[2]{0:T(128)S(1)} %get-tuple-element.10), channel_id=1, replica_groups=mesh['band'=2,'grid'=16] {'grid'}, use_global_device_ids=true, to_apply=%region_1.2 | all-reduce | flops 4 | bytes 32 | tf_op jit(solution)/shard_map/psum | solution.py:119
  194.7 2.3 multiply_subtract_fusion.1
  197.0 9.5 %multiply_reduce_fusion.3 = (f32[2]{0:T(128)S(1)}, f32[2,8,128,128,2]{3,4,2,1,0:T(2,128)S(1)}) fusion(f32[2,2,2]{2,1,0:T(2,128)S(1)} %copy-done.11, f32[2,2,8,128,128]{4,3,2,0,1:T(8,128)S(1)} %multiply_subtract_fusion.1), kind=kOutput, calls=%fused_computation.35 | convolution fusion | flops 13631486 | bytes 4195336 | tf_op jit(solution)/shard_map/ij,jcxyz->icxyz/dot_general | solution.py:128
  206.7 37.0 %all-reduce.1 = f32[32]{0:T(128)S(1)} all-reduce(f32[32]{0:T(128)S(1)} %dynamic-update-slice), channel_id=2, replica_groups=mesh['band'=2,'grid'=16] {'grid'}, use_global_device_ids=true, to_apply=%add.1 | all-reduce | flops 32 | bytes 256
  251.7 1.3 fusion.28
  253.0 1.3 fusion.29
  255.7 44.4 %all_to_all.127 = f32[2,2,8,128,128]{4,2,0,1,3:T(8,128)S(1)} all-to-all(f32[2,2,8,128,128]{4,2,0,1,3:T(8,128)S(1)} %copy.116), channel_id=1, replica_groups=mesh['band'=2,'grid'=16] {'grid'}, dimensions={3} | all-to-all | bytes 4194304 | tf_op jit(solution)/shard_map/all_to_all | solution.py:103
  303.0 1.3 fusion.26
  304.4 1.4 fusion.27
  308.6 1.3 fusion.24
  309.9 1.3 fusion.25
  312.7 45.8 %all_to_all.129 = f32[2,2,128,8,128]{4,3,0,1,2:T(8,128)S(1)} all-to-all(f32[2,2,128,8,128]{4,3,0,1,2:T(8,128)S(1)} %copy.118), channel_id=1, replica_groups=mesh['band'=2,'grid'=16] {'grid'}, dimensions={2} | all-to-all | bytes 4194304 | tf_op jit(solution)/shard_map/all_to_all | solution.py:106
  369.9 29.9 %all-reduce.3 = (f32[2]{0:T(128)S(1)}, f32[2]{0:T(128)S(1)}) all-reduce(f32[2]{0:T(128)S(1)} %get-tuple-element.9, f32[2]{0:T(128)S(1)} %get-tuple-element.8), channel_id=1, replica_groups=mesh['band'=2,'grid'=16] {'grid'}, use_global_device_ids=true, to_apply=%region_7.8 | all-reduce | flops 4 | bytes 32 | tf_op jit(solution)/shard_map/psum | solution.py:119
  399.8 2.3 multiply_subtract_fusion
  402.0 9.9 %multiply_reduce_fusion = (f32[2]{0:T(128)S(1)}, f32[2,8,128,128,2]{3,4,2,1,0:T(2,128)}) fusion(f32[2,2,2]{2,1,0:T(2,128)S(1)} %copy-done.11, f32[2,2,8,128,128]{4,3,2,0,1:T(8,128)S(1)} %multiply_subtract_fusion), kind=kOutput, calls=%fused_computation.31 | convolution fusion | flops 13631486 | bytes 4195336 | tf_op jit(solution)/shard_map/ij,jcxyz->icxyz/dot_general | solution.py:128
  412.2 36.7 %all-reduce.2 = f32[32]{0:T(128)S(1)} all-reduce(f32[32]{0:T(128)S(1)} %dynamic-update-slice.1), channel_id=3, replica_groups=mesh['band'=2,'grid'=16] {'grid'}, use_global_device_ids=true, to_apply=%add.2 | all-reduce | flops 32 | bytes 256
  449.0 2.6 divide_bitcast_fusion
  459.3 1.3 fusion.19
  460.6 1.3 fusion.18
  462.1 1.4 copy.133
  463.5 44.1 %all_to_all.128 = f32[2,2,8,128,128]{4,2,0,1,3:T(8,128)S(1)} all-to-all(f32[2,2,8,128,128]{4,2,0,1,3:T(8,128)S(1)} %copy.133), channel_id=1, replica_groups=mesh['band'=2,'grid'=16] {'grid'}, dimensions={3} | all-to-all | bytes 4194304 | tf_op jit(solution)/shard_map/all_to_all | solution.py:103
  511.8 1.3 fusion.17
  514.2 18.1 %all-reduce.7.cloned.1.call-done = f32[8,128,128]{2,1,0:T(8,128)} async-done(((f32[8,128,128]{2,1,0:T(8,128)}), f32[8,128,128]{2,1,0:T(8,128)}) %all-reduce.7.cloned.1.call-update) | async-done | bytes 524304 | tf_op jit(solution)/shard_map/psum | solution.py:136
  532.3 2.3 fusion.639
  538.2 1.6 copy.135
  539.7 7.3 %all-to-all-start.5 = ((f32[1,2,128,8,128]{4,3,1,0,2:T(8,128)}), f32[1,2,128,8,128]{4,3,1,0,2:T(8,128)}, u32[]{:S(2)}, u32[]{:S(2)}) async-start(f32[1,2,128,8,128]{4,3,1,0,2:T(8,128)} %copy.135), calls=%async_computation.5 | async-start | bytes 2097152 | tf_op jit(solution)/shard_map/all_to_all | solution.py:106
  547.1 25.3 %all-to-all-done.5 = f32[1,2,128,8,128]{4,3,1,0,2:T(8,128)} async-done(((f32[1,2,128,8,128]{4,3,1,0,2:T(8,128)}), f32[1,2,128,8,128]{4,3,1,0,2:T(8,128)}, u32[]{:S(2)}, u32[]{:S(2)}) %all-to-all-start.5) | async-done | bytes 1048608 | tf_op jit(solution)/shard_map/all_to_all | solution.py:106
  572.5 1.3 copy.255
  585.0 1.5 fusion.137
  589.0 1.3 fusion.15
  591.8 2.5 copy.145
  594.3 5.9 all-to-all-start.6
  600.3 1.6 copy.147
  601.9 45.7 %all-to-all-done.6 = f32[2,2,8,128,128]{4,2,0,1,3:T(8,128)} async-done(((f32[2,2,8,128,128]{4,2,0,1,3:T(8,128)}), f32[2,2,8,128,128]{4,2,0,1,3:T(8,128)}, u32[]{:S(2)}, u32[]{:S(2)}) %all-to-all-start.6) | async-done | bytes 2097184 | tf_op jit(solution)/shard_map/all_to_all | solution.py:103
  647.6 1.8 copy.249
  653.3 1.4 fusion.13
  655.4 4.3 add_tanh_fusion
  659.8 15.2 %fusion = f32[1,8,128,128]{3,0,2,1:T(1,128)S(1)} fusion(f32[32,8,128,128]{3,2,1,0:T(8,128)S(1)} %add_tanh_fusion, f32[32]{0:T(128)S(1)} %copy-done), kind=kOutput, calls=%fused_computation | convolution fusion | flops 50331648 | bytes 17301632 | tf_op jit(solution)/shard_map/k,kyxz->yxz/dot_general | solution.py:164
  (146 shorter events, 95.2 us)
Async XLA Ops:
  7.2 652.6 %copy-start = (f32[32]{0:T(128)S(1)}, f32[32]{0:T(128)}, u32[]{:S(2)}) copy-start(f32[32]{0:T(128)} %param.13) | copy-start | bytes 388
  79.8 1.4 copy-start.6
  89.4 16.9 %copy-start.12 = (u32[32]{0:T(128)S(1)}, u32[32]{0:T(128)}, u32[]{:S(2)}) copy-start(u32[32]{0:T(128)} %constant.105) | copy-start | bytes 388
  89.4 63.6 %all-to-all-start.1 = ((f32[2,2,128,8,128]{4,3,0,1,2:T(8,128)}), f32[2,2,128,8,128]{4,3,0,1,2:T(8,128)S(1)}, u32[]{:S(2)}, u32[]{:S(2)}) async-start(f32[2,2,128,8,128]{4,3,0,1,2:T(8,128)} %copy.104), calls=%async_computation.1 | async-start | bytes 4194304 | tf_op jit(solution)/shard_map/all_to_all | solution.py:106
  106.3 426.0 %all-reduce.7.cloned.1.call-start = ((), (), s32[]{:S(2)}) async-start(), calls=%async_computation.7 | async-start | bytes 1048576 | tf_op jit(solution)/shard_map/psum | solution.py:136
  162.2 2.9 copy-start.4
  162.2 2.0 copy-start.1
  164.2 1.0 copy-start.5
  194.7 2.3 copy-start.11
  304.4 1.4 copy-start.7
  367.6 2.3 copy-start.2
  368.9 1.1 copy-start.3
  513.1 19.1 %copy-start.9 = (f32[8,128,128]{2,1,0:T(8,128)S(1)}, f32[8,128,128]{2,1,0:T(8,128)}, u32[]{:S(2)}) copy-start(f32[8,128,128]{2,1,0:T(8,128)} %param.10) | copy-start | bytes 1572868
  539.7 32.7 %all-to-all-start.5 = ((f32[1,2,128,8,128]{4,3,1,0,2:T(8,128)}), f32[1,2,128,8,128]{4,3,1,0,2:T(8,128)}, u32[]{:S(2)}, u32[]{:S(2)}) async-start(f32[1,2,128,8,128]{4,3,1,0,2:T(8,128)} %copy.135), calls=%async_computation.5 | async-start | bytes 2097152 | tf_op jit(solution)/shard_map/all_to_all | solution.py:106
  594.3 6.0 copy-start.10
  594.3 53.2 %all-to-all-start.6 = ((f32[2,2,8,128,128]{4,2,0,1,3:T(8,128)}), f32[2,2,8,128,128]{4,2,0,1,3:T(8,128)}, u32[]{:S(2)}, u32[]{:S(2)}) async-start(f32[2,2,8,128,128]{4,2,0,1,3:T(8,128)} %copy.145), calls=%async_computation.6 | async-start | bytes 4194304 | tf_op jit(solution)/shard_map/all_to_all | solution.py:103
  659.8 15.3 %copy-start.8 = (f32[8,128,128]{2,1,0:T(8,128)S(1)}, f32[8,128,128]{2,1,0:T(8,128)}, u32[]{:S(2)}) copy-start(f32[8,128,128]{2,1,0:T(8,128)} %param.9) | copy-start | bytes 1572868
Sparse Core Ops, SparseCore 0:
  514.3 17.9 all-reduce.6
